TPU v7x, 32 devices: a whole 2x2x4 slice. The times are simulated.
32 devices in a mesh: row: 8 (over y, x, core), col: 4 (over z).
Axes of the slice: x: 2, y: 2, z: 4, core: 2. Of those that a mesh axis runs over, the one named last changes fastest.
Arguments:
- act_tiles: bfloat16 [3072, 2048], P('row', 'col'), may hold values from -6 to 6
- up_tiles: bfloat16 [2048, 3584], P('row', 'col'), may hold values from -0.125 to 0.125
Outputs:
- hidden_act: bfloat16 [3072, 3584], P('row', 'col')
All inputs are finite; a program needn't handle non-finite values.
Results may differ from a plain program's by a relative error of at most 0.001.
Values may be sent and summed in bfloat16 or wider, within the bound.
A program may use at most 64 MiB of HBM per device.

v0:
```python
import functools

import jax
import jax.numpy as jnp
from jax import lax
from jax.experimental import pallas as pl
from jax.experimental.pallas import tpu as pltpu
from jax.sharding import PartitionSpec as P

MESH = pl.DeviceIdType.MESH


def pieces_of(rows, wanted, multiple):
    return max(n for n in range(1, wanted + 1) if rows % (n * multiple) == 0)


def pieces_halved(rows, wanted, multiple):
    pieces = []
    while len(pieces) < wanted - 1 and rows % (2 * multiple) == 0:
        rows //= 2
        pieces.append(rows)
    return pieces + [rows]


def kernel(grid, counts, a_hbm, w_hbm, out, acts, weights, total, send_a, recv_a, send_w, recv_w, share_w, local_sem, go):
    n_y, n_x, n_col = grid
    n_a, n_w = counts
    n_row = 2 * n_y * n_x
    tokens, width = acts.shape[1:]
    depth, hidden = weights.shape[1:]
    per = width // depth
    row_w = depth // n_w
    starts_a = [sum(n_a[:k]) for k in range(len(n_a))]
    sizes_a, n_a = n_a, len(n_a)

    r, c = lax.axis_index("row"), lax.axis_index("col")
    core = lax.rem(r, 2)
    x = lax.rem(r // 2, n_x)
    y = r // (2 * n_x)
    last = n_col - 1

    def row_of(dy, dx, other_core=False):
        which = 1 - core if other_core else core
        return (lax.rem(y + dy, n_y) * n_x + lax.rem(x + dx, n_x)) * 2 + which

    pair = row_of(0, 0, True)
    peers_x = [(0, dx) for dx in range(1, n_x)]
    peers_y = [(dy, 0) for dy in range(1, n_y)]
    diagonal = [(dy, dx) for dy in range(1, n_y) for dx in range(1, n_x)]
    near = [row_of(*p) for p in peers_x + peers_y]
    far = [row_of(*p) for p in diagonal]
    row_peers = near + [pair]

    def weight_at(source, owner, k):
        rel = lax.rem(source - owner + n_row, n_row)
        return weights.at[rel, pl.ds(k * row_w, row_w)]

    def weight_copy(source, to, recv, k, own=False):
        return pltpu.make_async_remote_copy(
            src_ref=w_hbm.at[pl.ds(k * row_w, row_w)] if own else weight_at(source, r, k),
            dst_ref=weight_at(source, to, k),
            send_sem=send_w,
            recv_sem=recv,
            device_id=(to, c),
            device_id_type=MESH,
        )

    def act_copy(source, side, k, own=False):
        rows = pl.ds(starts_a[k], sizes_a[k])
        return pltpu.make_async_remote_copy(
            src_ref=a_hbm.at[rows] if own else acts.at[source, rows],
            dst_ref=acts.at[source, rows],
            send_sem=send_a.at[side],
            recv_sem=recv_a.at[source, k],
            device_id=(r, c + 2 * side - 1),
            device_id_type=MESH,
        )

    def filled(ref, sem):
        pltpu.make_async_copy(ref, ref, sem).wait()

    barrier = pltpu.get_barrier_semaphore()

    def greet(to):
        pl.semaphore_signal(barrier, inc=1, device_id=to, device_id_type=MESH)

    def tell(to):
        pl.semaphore_signal(go, inc=1, device_id=to, device_id_type=MESH)

    early = c == 1

    @pl.when(jnp.logical_and(c < last, c != 0))
    def _():
        greet((r, c + 1))

    @pl.when(jnp.logical_and(c > 0, c != 2))
    def _():
        greet((r, c - 1))

    @pl.when(jnp.logical_and(c == 0, c < last))
    def _():
        greet((r, c + 1))

    @pl.when(jnp.logical_not(early))
    def _():
        for to in row_peers:
            greet((to, c))

    own_a = pltpu.make_async_copy(a_hbm, acts.at[c], local_sem.at[0])
    own_w = pltpu.make_async_copy(w_hbm, weights.at[0], local_sem.at[1])
    own_a.start()
    own_w.start()

    def own_acts(side):
        for k in range(n_a):
            act_copy(c, side, k, True).start()

    @pl.when(early)
    def _():
        pl.semaphore_wait(barrier, 1)
        own_acts(0)
        pl.semaphore_wait(go, 2 if n_col > 2 else 1)

    @pl.when(jnp.logical_not(early))
    def _():
        beside = jnp.where(c > 0, 1, 0) + jnp.where(c < last, 1, 0)
        pl.semaphore_wait(barrier, len(row_peers) + beside)

        @pl.when(c > 0)
        def _():
            own_acts(0)

        @pl.when(c == 2)
        def _():
            tell((r, c - 1))

    @pl.when(jnp.logical_and(c == 0, c < last))
    def _():
        for to in row_peers:
            tell((to, c))

    @pl.when(c < last)
    def _():
        own_acts(1)

    for k in range(n_w):
        for to in near:
            weight_copy(r, to, recv_w.at[0, k], k, True).start()
        weight_copy(r, pair, share_w, k, True).start()

    @pl.when(jnp.logical_and(c == 0, c < last))
    def _():
        pl.semaphore_wait(go, len(row_peers))
        tell((r, c + 1))

    def first_weights(k):
        filled(weights.at[pl.ds(0, len(near)), pl.ds(0, row_w)], recv_w.at[0, k])
        for dy, dx in diagonal:
            @pl.when(core == 0)
            def _():
                weight_copy(row_of(dy, 0), row_of(0, dx), recv_w.at[1, k], k).start()

            @pl.when(core == 1)
            def _():
                weight_copy(row_of(0, dx), row_of(dy, 0), recv_w.at[1, k], k).start()
        for source in near:
            weight_copy(source, pair, share_w, k).start()

    def far_weights(k):
        filled(weights.at[pl.ds(0, len(far)), pl.ds(0, row_w)], recv_w.at[1, k])
        for source in far:
            weight_copy(source, pair, share_w, k).start()

    short = jnp.minimum(c, last - c)
    toward = jnp.where(last - c >= c, 1, -1)

    def source_at(t):
        near_step = t // 2 + 1
        near_sign = toward * (1 - 2 * lax.rem(t, 2))
        return jnp.where(t < 2 * short, c + near_sign * near_step, c + toward * (t - short + 1))

    inner = jnp.logical_and(c > 0, c < last)

    def pass_acts(t, k):
        source = source_at(t)
        act_copy(source, 0, k).wait_recv()

        @pl.when(source < c)
        def _():
            act_copy(source, 1, k).start()

        @pl.when(source > c)
        def _():
            act_copy(source, 0, k).start()

    events = []
    a_time, w_time = tokens // n_a * width, row_w * hidden
    for t in range(last):
        for k in range(n_a):
            events.append(((t // 2 * n_a + k + 1) * a_time, "a", t, k))
    for k in range(n_w):
        events.append(((k + 1) * w_time * (n_x + n_y - 2) / 2, "near", 0, k))
        events.append(((k + 2) * w_time * (n_x + n_y - 2) / 2 + w_time, "far", 0, k))
    for _, kind, t, k in sorted(events):
        if kind == "a":
            pl.when(inner)(functools.partial(pass_acts, t, k))
        elif kind == "near":
            first_weights(k)
        elif diagonal:
            far_weights(k)
    filled(weights.at[pl.ds(0, n_row // 2)], share_w)
    own_w.wait()
    own_a.wait()

    def product(source, rows):
        at = lax.rem(source - c + n_col, n_col)
        held = weights[pl.ds(at * per, per)].reshape(width, hidden)
        return jnp.dot(acts[source, rows, :], held, preferred_element_type=jnp.float32)

    every = pl.ds(0, tokens)
    total[...] = product(c, every)

    @pl.loop(0, last - 1)
    def _(t):
        source = source_at(t)

        @pl.when(jnp.logical_not(inner))
        def _():
            for k in range(n_a):
                act_copy(source, 0, k).wait_recv()

        total[...] += product(source, every)

    final = source_at(last - 1)

    for k in range(n_a):
        rows = pl.ds(starts_a[k], sizes_a[k])

        pl.when(jnp.logical_not(inner))(act_copy(final, 0, k).wait_recv)

        pre = total[rows, :] + product(final, rows)
        out[rows, :] = (pre / (1.0 + jnp.exp(-pre))).astype(out.dtype)

    for n in range(1, n_col):
        pl.when(jnp.logical_and(c < last, c + 1 == n))(functools.partial(filled, acts.at[pl.ds(0, n)], send_a.at[1]))
        pl.when(jnp.logical_and(c > 0, n_col - c == n))(functools.partial(filled, acts.at[pl.ds(0, n)], send_a.at[0]))
    filled(weights.at[pl.ds(0, n_row - 1)], send_w)


def body(n_row, n_col, act_tiles, up_tiles):
    tokens, width = act_tiles.shape
    depth, hidden = up_tiles.shape
    chips = n_row // 2
    n_x = max(n for n in range(1, chips + 1) if chips % n == 0 and n * n <= chips)
    n_y = chips // n_x
    cuts, n_w = pieces_halved(tokens, 3, 16), pieces_of(depth, 2, 16)
    n_a = len(cuts)
    return pl.pallas_call(
        functools.partial(kernel, (n_y, n_x, n_col), (cuts, n_w)),
        out_shape=pltpu.VMEM((tokens, hidden), jnp.bfloat16),
        in_specs=[pl.BlockSpec(memory_space=pltpu.HBM)] * 2,
        out_specs=pl.BlockSpec(memory_space=pltpu.VMEM),
        scratch_shapes=[
            pltpu.VMEM((n_col, tokens, width), jnp.bfloat16),
            pltpu.VMEM((n_row, depth, hidden), jnp.bfloat16),
            pltpu.VMEM((tokens, hidden), jnp.float32),
            pltpu.SemaphoreType.DMA((2,)),
            pltpu.SemaphoreType.DMA((n_col, n_a)),
            pltpu.SemaphoreType.DMA,
            pltpu.SemaphoreType.DMA((2, n_w)),
            pltpu.SemaphoreType.DMA,
            pltpu.SemaphoreType.DMA((2,)),
            pltpu.SemaphoreType.REGULAR,
        ],
        compiler_params=pltpu.CompilerParams(collective_id=0, has_side_effects=True, vmem_limit_bytes=60000000),
        cost_estimate=pl.CostEstimate(
            flops=2 * tokens * width * n_col * hidden,
            bytes_accessed=2 * (act_tiles.size + up_tiles.size + tokens * hidden),
            transcendentals=tokens * hidden,
        ),
        name="gather_up_silu",
    )(act_tiles, up_tiles)


def solution(mesh):
    return jax.shard_map(
        functools.partial(body, mesh.shape["row"], mesh.shape["col"]),
        mesh=mesh,
        in_specs=(P("row", "col"), P("row", "col")),
        out_specs=P("row", "col"),
        check_vma=False,
    )
```

profile of v0, /device:TPU:0, one launch (start us, length us, event | category | flops | bytes accessed | tf_op | source)
XLA Modules:
  0.0 30.7 jit_solution(8806661629724738498)
XLA Ops:
  0.0 29.8 %gather_up_silu.1 = bf16[384,896]{1,0:T(8,128)(2,1)S(1)} custom-call(bf16[384,512]{1,0:T(8,128)(2,1)} %a_hbm.1, bf16[256,896]{1,0:T(8,128)(2,1)} %w_hbm.1), custom_call_target="tpu_custom_call" | custom-call | flops 1409286144 | bytes 1540096 | tf_op jit(solution)/shard_map/gather_up_silu/pallas_call | solution.py:258
  29.8 0.8 %copy.4 = bf16[384,896]{1,0:T(8,128)(2,1)} copy(bf16[384,896]{1,0:T(8,128)(2,1)S(1)} %gather_up_silu.1) | data formatting | bytes 1376256
where the time goes:
time: 30.8 us; the launch traced here: 30.7 us
  Pallas kernels  29.8 us (97%)
  local copies, waits for them, and re-layouts  0.85 us (3%)
    pallas_call x1, Pallas kernels, body(): pl.pallas_call(functools.partial(kernel, (n_y, n_x, n_col), (cuts, n_w)),...  29.8 us
    unnamed x1, local copies, waits for them, and re-layouts  0.85 us

commit v1 on v0

--- a/solution.py
+++ b/solution.py
@@ -14,15 +14,12 @@
     return max(n for n in range(1, wanted + 1) if rows % (n * multiple) == 0)
 
 
-def pieces_halved(rows, wanted, multiple):
-    pieces = []
-    while len(pieces) < wanted - 1 and rows % (2 * multiple) == 0:
-        rows //= 2
-        pieces.append(rows)
-    return pieces + [rows]
-
-
-def kernel(grid, counts, a_hbm, w_hbm, out, acts, weights, total, send_a, recv_a, send_w, recv_w, share_w, local_sem, go):
+def pieces_uneven(rows, shares, multiple):
+    unit = rows // sum(shares)
+    return [n * unit for n in shares] if unit * sum(shares) == rows and unit % multiple == 0 else [rows]
+
+
+def kernel(grid, counts, a_hbm, w_hbm, out, acts, weights, total, send_a, recv_a, send_w, recv_w, share_w, local_sem, go, held, send_h, recv_h):
     n_y, n_x, n_col = grid
     n_a, n_w = counts
     n_row = 2 * n_y * n_x
@@ -51,6 +48,11 @@
     far = [row_of(*p) for p in diagonal]
     row_peers = near + [pair]
 
+    helpers = []
+    if n_a > 2 and n_col > 1:
+        helpers += [(3, n_a - 2)] if n_x > 1 else []
+        helpers += [(2 * n_x + 1, n_a - 1)] if n_y > 1 else []
+
     def weight_at(source, owner, k):
         rel = lax.rem(source - owner + n_row, n_row)
         return weights.at[rel, pl.ds(k * row_w, row_w)]
@@ -65,17 +67,26 @@
             device_id_type=MESH,
         )
 
-    def act_copy(source, side, k, own=False):
+    def act_copy(source, side, k, own=False, arrives=False):
+        to = c if arrives else c + 2 * side - 1
         rows = pl.ds(starts_a[k], sizes_a[k])
         return pltpu.make_async_remote_copy(
             src_ref=a_hbm.at[rows] if own else acts.at[source, rows],
             dst_ref=acts.at[source, rows],
             send_sem=send_a.at[side],
-            recv_sem=recv_a.at[source, k],
-            device_id=(r, c + 2 * side - 1),
+            recv_sem=recv_a.at[lax.rem(source - to + n_col, n_col) - 1, k],
+            device_id=(r, to),
             device_id_type=MESH,
         )
 
+    def held_copy(src, dst, to, send, recv):
+        return pltpu.make_async_remote_copy(
+            src_ref=src, dst_ref=dst, send_sem=send, recv_sem=recv, device_id=to, device_id_type=MESH
+        )
+
+    def wait_acts(source, k):
+        act_copy(source, 0, k, arrives=True).wait_recv()
+
     def filled(ref, sem):
         pltpu.make_async_copy(ref, ref, sem).wait()
 
@@ -105,6 +116,18 @@
     def _():
         for to in row_peers:
             greet((to, c))
+
+    for helper, _ in helpers:
+        @pl.when(jnp.logical_and(c == 0, r == 0))
+        def _():
+            greet((helper, 0))
+
+        @pl.when(jnp.logical_and(c == 0, r == helper))
+        def _():
+            greet((0, 0))
+
+    helped = jnp.where(r == 0, len(helpers), sum((jnp.where(r == helper, 1, 0) for helper, _ in helpers), 0))
+    helped = jnp.where(c == 0, helped, 0)
 
     own_a = pltpu.make_async_copy(a_hbm, acts.at[c], local_sem.at[0])
     own_w = pltpu.make_async_copy(w_hbm, weights.at[0], local_sem.at[1])
@@ -118,13 +141,22 @@
     @pl.when(early)
     def _():
         pl.semaphore_wait(barrier, 1)
-        own_acts(0)
+        for k in range(n_a):
+            if k in [taken for _, taken in helpers]:
+                pl.when(r != 0)(act_copy(c, 0, k, True).start)
+            else:
+                act_copy(c, 0, k, True).start()
         pl.semaphore_wait(go, 2 if n_col > 2 else 1)
 
+        @pl.when(r == 0)
+        def _():
+            for helper, k in helpers:
+                held_copy(a_hbm.at[pl.ds(starts_a[k], sizes_a[k])], held, (helper, 1), send_a.at[0], recv_h).start()
+
     @pl.when(jnp.logical_not(early))
     def _():
         beside = jnp.where(c > 0, 1, 0) + jnp.where(c < last, 1, 0)
-        pl.semaphore_wait(barrier, len(row_peers) + beside)
+        pl.semaphore_wait(barrier, len(row_peers) + beside + helped)
 
         @pl.when(c > 0)
         def _():
@@ -138,6 +170,8 @@
     def _():
         for to in row_peers:
             tell((to, c))
+        for helper, _ in helpers:
+            pl.when(r == helper)(functools.partial(tell, (0, c)))
 
     @pl.when(c < last)
     def _():
@@ -150,7 +184,7 @@
 
     @pl.when(jnp.logical_and(c == 0, c < last))
     def _():
-        pl.semaphore_wait(go, len(row_peers))
+        pl.semaphore_wait(go, len(row_peers) + jnp.where(r == 0, len(helpers), 0))
         tell((r, c + 1))
 
     def first_weights(k):
@@ -183,7 +217,7 @@
 
     def pass_acts(t, k):
         source = source_at(t)
-        act_copy(source, 0, k).wait_recv()
+        wait_acts(source, k)
 
         @pl.when(source < c)
         def _():
@@ -193,17 +227,36 @@
         def _():
             act_copy(source, 0, k).start()
 
-    events = []
-    a_time, w_time = tokens // n_a * width, row_w * hidden
+    def help_out():
+        for helper, k in helpers:
+            @pl.when(jnp.logical_and(c == 1, r == helper))
+            def _():
+                filled(held, recv_h)
+                held_copy(held, held, (r, 0), send_h, recv_h).start()
+
+    def help_in():
+        for helper, k in helpers:
+            @pl.when(jnp.logical_and(c == 0, r == helper))
+            def _():
+                filled(held, recv_h)
+                there = acts.at[1, pl.ds(starts_a[k], sizes_a[k])]
+                held_copy(held, there, (0, 0), send_h, recv_a.at[0, k]).start()
+
+    events = [(0.4 * tokens * width, "out", 0, 0), (1.1 * tokens * width, "in", 0, 0)]
+    w_time, w_lag = row_w * hidden, tokens * width / 10
     for t in range(last):
         for k in range(n_a):
-            events.append(((t // 2 * n_a + k + 1) * a_time, "a", t, k))
+            events.append(((t // 2 * tokens + starts_a[k] + sizes_a[k]) * width, "a", t, k))
     for k in range(n_w):
-        events.append(((k + 1) * w_time * (n_x + n_y - 2) / 2, "near", 0, k))
-        events.append(((k + 2) * w_time * (n_x + n_y - 2) / 2 + w_time, "far", 0, k))
+        events.append(((k + 1) * w_time * (n_x + n_y - 2) / 2 + w_lag, "near", 0, k))
+        events.append(((k + 2) * w_time * (n_x + n_y - 2) / 2 + w_time + w_lag, "far", 0, k))
     for _, kind, t, k in sorted(events):
         if kind == "a":
             pl.when(inner)(functools.partial(pass_acts, t, k))
+        elif kind == "out":
+            help_out()
+        elif kind == "in":
+            help_in()
         elif kind == "near":
             first_weights(k)
         elif diagonal:
@@ -227,7 +280,7 @@
         @pl.when(jnp.logical_not(inner))
         def _():
             for k in range(n_a):
-                act_copy(source, 0, k).wait_recv()
+                wait_acts(source, k)
 
         total[...] += product(source, every)
 
@@ -236,7 +289,7 @@
     for k in range(n_a):
         rows = pl.ds(starts_a[k], sizes_a[k])
 
-        pl.when(jnp.logical_not(inner))(act_copy(final, 0, k).wait_recv)
+        pl.when(jnp.logical_not(inner))(functools.partial(wait_acts, final, k))
 
         pre = total[rows, :] + product(final, rows)
         out[rows, :] = (pre / (1.0 + jnp.exp(-pre))).astype(out.dtype)
@@ -244,6 +297,8 @@
     for n in range(1, n_col):
         pl.when(jnp.logical_and(c < last, c + 1 == n))(functools.partial(filled, acts.at[pl.ds(0, n)], send_a.at[1]))
         pl.when(jnp.logical_and(c > 0, n_col - c == n))(functools.partial(filled, acts.at[pl.ds(0, n)], send_a.at[0]))
+    for helper, _ in helpers:
+        pl.when(jnp.logical_and(c < 2, r == helper))(functools.partial(filled, held, send_h))
     filled(weights.at[pl.ds(0, n_row - 1)], send_w)
 
 
@@ -253,7 +308,7 @@
     chips = n_row // 2
     n_x = max(n for n in range(1, chips + 1) if chips % n == 0 and n * n <= chips)
     n_y = chips // n_x
-    cuts, n_w = pieces_halved(tokens, 3, 16), pieces_of(depth, 2, 16)
+    cuts, n_w = pieces_uneven(tokens, (2, 4, 1, 1), 16), pieces_of(depth, 2, 16)
     n_a = len(cuts)
     return pl.pallas_call(
         functools.partial(kernel, (n_y, n_x, n_col), (cuts, n_w)),
@@ -265,12 +320,15 @@
             pltpu.VMEM((n_row, depth, hidden), jnp.bfloat16),
             pltpu.VMEM((tokens, hidden), jnp.float32),
             pltpu.SemaphoreType.DMA((2,)),
-            pltpu.SemaphoreType.DMA((n_col, n_a)),
+            pltpu.SemaphoreType.DMA((max(n_col - 1, 1), n_a)),
             pltpu.SemaphoreType.DMA,
             pltpu.SemaphoreType.DMA((2, n_w)),
             pltpu.SemaphoreType.DMA,
             pltpu.SemaphoreType.DMA((2,)),
             pltpu.SemaphoreType.REGULAR,
+            pltpu.VMEM((cuts[-1], width), jnp.bfloat16),
+            pltpu.SemaphoreType.DMA,
+            pltpu.SemaphoreType.DMA,
         ],
         compiler_params=pltpu.CompilerParams(collective_id=0, has_side_effects=True, vmem_limit_bytes=60000000),
         cost_estimate=pl.CostEstimate(

time: 30.8 us -> 30 us (0.974)
  Pallas kernels: 29.8 us -> 28.7 us
    pallas_call x1, Pallas kernels: 29.8 us -> 28.7 us  [body(): pl.pallas_call(functools.partial(kernel, (n_y, n_x, n_col), (cuts, n_w)),...]
where the time goes in v1:
time: 30 us; the launch traced here: 29.6 us
  Pallas kernels  28.7 us (96%)
  local copies, waits for them, and re-layouts  0.85 us (3%)
    pallas_call x1, Pallas kernels, body(): pl.pallas_call(functools.partial(kernel, (n_y, n_x, n_col), (cuts, n_w)),...  28.7 us
    unnamed x1, local copies, waits for them, and re-layouts  0.85 us

profile of v1, /device:TPU:0, one launch (start us, length us, event | category | flops | bytes accessed | tf_op | source)
XLA Modules:
  0.0 29.6 jit_solution(5047799820727121206)
XLA Ops:
  0.0 28.7 %gather_up_silu.1 = bf16[384,896]{1,0:T(8,128)(2,1)S(1)} custom-call(bf16[384,512]{1,0:T(8,128)(2,1)} %a_hbm.1, bf16[256,896]{1,0:T(8,128)(2,1)} %w_hbm.1), custom_call_target="tpu_custom_call" | custom-call | flops 1409286144 | bytes 1540096 | tf_op jit(solution)/shard_map/gather_up_silu/pallas_call | solution.py:313
  28.7 0.8 %copy.4 = bf16[384,896]{1,0:T(8,128)(2,1)} copy(bf16[384,896]{1,0:T(8,128)(2,1)S(1)} %gather_up_silu.1) | data formatting | bytes 1376256

commit v2 on v1

--- a/solution.py
+++ b/solution.py
@@ -17,6 +17,40 @@
 def pieces_uneven(rows, shares, multiple):
     unit = rows // sum(shares)
     return [n * unit for n in shares] if unit * sum(shares) == rows and unit % multiple == 0 else [rows]
+
+
+def nth_source(n_col, c, t):
+    last = n_col - 1
+    short = jnp.minimum(c, last - c)
+    toward = jnp.where(last - c >= c, 1, -1)
+    near_step = t // 2 + 1
+    near_sign = toward * (1 - 2 * lax.rem(t, 2))
+    return jnp.where(t < 2 * short, c + near_sign * near_step, c + toward * (t - short + 1))
+
+
+def product_of(n_col, c, acts, weights, source, rows):
+    width, (depth, hidden) = acts.shape[2], weights.shape[1:]
+    per = width // depth
+    at = lax.rem(source - c + n_col, n_col)
+    held = weights[pl.ds(at * per, per)].reshape(width, hidden)
+    return jnp.dot(acts[source, rows, :], held, preferred_element_type=jnp.float32)
+
+
+def finish(n_col, start, ready, acts, weights, total, out, tail, sems):
+    c = lax.axis_index("col")
+    size = tail.shape[0]
+    rows = pl.ds(start, size)
+    head = pl.ds(0, start)
+    first = pltpu.make_async_copy(ready.at[head], out.at[head], sems.at[0])
+    if start:
+        first.start()
+    pre = total[rows, :] + product_of(n_col, c, acts, weights, nth_source(n_col, c, n_col - 2), rows)
+    tail[...] = (pre / (1.0 + jnp.exp(-pre))).astype(out.dtype)
+    second = pltpu.make_async_copy(tail, out.at[rows], sems.at[1])
+    second.start()
+    if start:
+        first.wait()
+    second.wait()
 
 
 def kernel(grid, counts, a_hbm, w_hbm, out, acts, weights, total, send_a, recv_a, send_w, recv_w, share_w, local_sem, go, held, send_h, recv_h):
@@ -205,14 +239,7 @@
         for source in far:
             weight_copy(source, pair, share_w, k).start()
 
-    short = jnp.minimum(c, last - c)
-    toward = jnp.where(last - c >= c, 1, -1)
-
-    def source_at(t):
-        near_step = t // 2 + 1
-        near_sign = toward * (1 - 2 * lax.rem(t, 2))
-        return jnp.where(t < 2 * short, c + near_sign * near_step, c + toward * (t - short + 1))
-
+    source_at = functools.partial(nth_source, n_col, c)
     inner = jnp.logical_and(c > 0, c < last)
 
     def pass_acts(t, k):
@@ -265,10 +292,7 @@
     own_w.wait()
     own_a.wait()
 
-    def product(source, rows):
-        at = lax.rem(source - c + n_col, n_col)
-        held = weights[pl.ds(at * per, per)].reshape(width, hidden)
-        return jnp.dot(acts[source, rows, :], held, preferred_element_type=jnp.float32)
+    product = functools.partial(product_of, n_col, c, acts, weights)
 
     every = pl.ds(0, tokens)
     total[...] = product(c, every)
@@ -291,6 +315,8 @@
 
         pl.when(jnp.logical_not(inner))(functools.partial(wait_acts, final, k))
 
+        if k == n_a - 1:
+            break
         pre = total[rows, :] + product(final, rows)
         out[rows, :] = (pre / (1.0 + jnp.exp(-pre))).astype(out.dtype)
 
@@ -310,15 +336,17 @@
     n_y = chips // n_x
     cuts, n_w = pieces_uneven(tokens, (2, 4, 1, 1), 16), pieces_of(depth, 2, 16)
     n_a = len(cuts)
-    return pl.pallas_call(
+    held = pl.pallas_call(
         functools.partial(kernel, (n_y, n_x, n_col), (cuts, n_w)),
-        out_shape=pltpu.VMEM((tokens, hidden), jnp.bfloat16),
-        in_specs=[pl.BlockSpec(memory_space=pltpu.HBM)] * 2,
-        out_specs=pl.BlockSpec(memory_space=pltpu.VMEM),
-        scratch_shapes=[
+        out_shape=(
+            pltpu.VMEM((tokens, hidden), jnp.bfloat16),
             pltpu.VMEM((n_col, tokens, width), jnp.bfloat16),
             pltpu.VMEM((n_row, depth, hidden), jnp.bfloat16),
             pltpu.VMEM((tokens, hidden), jnp.float32),
+        ),
+        in_specs=[pl.BlockSpec(memory_space=pltpu.HBM)] * 2,
+        out_specs=(pl.BlockSpec(memory_space=pltpu.VMEM),) * 4,
+        scratch_shapes=[
             pltpu.SemaphoreType.DMA((2,)),
             pltpu.SemaphoreType.DMA((max(n_col - 1, 1), n_a)),
             pltpu.SemaphoreType.DMA,
@@ -330,14 +358,23 @@
             pltpu.SemaphoreType.DMA,
             pltpu.SemaphoreType.DMA,
         ],
-        compiler_params=pltpu.CompilerParams(collective_id=0, has_side_effects=True, vmem_limit_bytes=60000000),
+        compiler_params=pltpu.CompilerParams(collective_id=0, has_side_effects=True, vmem_limit_bytes=8000000),
         cost_estimate=pl.CostEstimate(
             flops=2 * tokens * width * n_col * hidden,
             bytes_accessed=2 * (act_tiles.size + up_tiles.size + tokens * hidden),
             transcendentals=tokens * hidden,
         ),
         name="gather_up_silu",
-    )(act_tiles, up_tiles)
+    )(*[pltpu.with_memory_space_constraint(a, pltpu.HBM) for a in (act_tiles, up_tiles)])
+    return pl.pallas_call(
+        functools.partial(finish, n_col, tokens - cuts[-1]),
+        out_shape=jax.ShapeDtypeStruct((tokens, hidden), jnp.bfloat16),
+        in_specs=[pl.BlockSpec(memory_space=pltpu.VMEM)] * 4,
+        out_specs=pl.BlockSpec(memory_space=pltpu.HBM),
+        scratch_shapes=[pltpu.VMEM((cuts[-1], hidden), jnp.bfloat16), pltpu.SemaphoreType.DMA((2,))],
+        compiler_params=pltpu.CompilerParams(vmem_limit_bytes=8000000),
+        name="last_rows",
+    )(*[pltpu.with_memory_space_constraint(a, pltpu.VMEM) for a in held])
 
 
 def solution(mesh):

time: 30 us -> 29.8 us (level)
  local copies, waits for them, and re-layouts: 0.85 us -> 0 us
  Pallas kernels: 28.7 us -> 29.4 us
    pallas_call x0 -> x1, Pallas kernels: none -> 0.97 us  [body(): pl.pallas_call(functools.partial(finish, n_col, tokens - cuts[-1]), out_s...]
    unnamed x1 -> x0, local copies, waits for them, and re-layouts: 0.85 us -> none
    pallas_call x1, Pallas kernels: 28.7 us -> 28.4 us  [body(): pl.pallas_call(functools.partial(kernel, (n_y, n_x, n_col), (cuts, n_w)),...]
where the time goes in v2:
time: 29.8 us; the launch traced here: 29.4 us
  Pallas kernels  29.4 us (99%)
    pallas_call x1, Pallas kernels, body(): pl.pallas_call(functools.partial(kernel, (n_y, n_x, n_col), (cuts, n_w)),...  28.4 us
    pallas_call x1, Pallas kernels, body(): pl.pallas_call(functools.partial(finish, n_col, tokens - cuts[-1]), out_s...  0.97 us

profile of v2, /device:TPU:0, one launch (start us, length us, event | category | flops | bytes accessed | tf_op | source)
XLA Modules:
  0.0 29.4 jit_solution(4871723655533106839)
XLA Ops:
  0.0 28.4 %gather_up_silu.1 = (bf16[384,896]{1,0:T(8,128)(2,1)S(1)}, bf16[4,384,512]{2,1,0:T(8,128)(2,1)S(1)}, bf16[8,256,896]{2,1,0:T(8,128)(2,1)S(1)}, f32[384,896]{1,0:T(8,128)S(1)}) custom-call(bf16[384,512]{1,0:T(8,128)(2,1)} %a_hbm.1, bf16[256,896]{1,0:T(8,128)(2,1)} %w_hbm.1), custom_call_target="tpu_custom_call" | custom-call | flops 1409286144 | bytes 1540096 | tf_op jit(solution)/shard_map/gather_up_silu/pallas_call | solution.py:339
  28.4 1.0 %last_rows.1 = bf16[384,896]{1,0:T(8,128)(2,1)} custom-call(bf16[384,896]{1,0:T(8,128)(2,1)S(1)} %get-tuple-element.9.ready, bf16[4,384,512]{2,1,0:T(8,128)(2,1)S(1)} %get-tuple-element.10.acts, bf16[8,256,896]{2,1,0:T(8,128)(2,1)S(1)} %get-tuple-element.11.weights, f32[384,896]{1,0:T(8,128)S(1)} %get-tuple-element.12.total), custom_call_target="tpu_custom_call" | custom-call | tf_op jit(solution)/shard_map/last_rows/pallas_call | solution.py:369

commit v3 on v2

--- a/solution.py
+++ b/solution.py
@@ -83,9 +83,10 @@
     row_peers = near + [pair]
 
     helpers = []
-    if n_a > 2 and n_col > 1:
-        helpers += [(3, n_a - 2)] if n_x > 1 else []
-        helpers += [(2 * n_x + 1, n_a - 1)] if n_y > 1 else []
+    if n_a > 3 and n_col > 1:
+        helpers += [(3, n_a - 3)] if n_x > 1 else []
+        helpers += [(2 * n_x + 1, n_a - 2)] if n_y > 1 else []
+        helpers += [(2 * n_x + 3, n_a - 1)] if n_x > 1 and n_y > 1 else []
 
     def weight_at(source, owner, k):
         rel = lax.rem(source - owner + n_row, n_row)
@@ -334,7 +335,7 @@
     chips = n_row // 2
     n_x = max(n for n in range(1, chips + 1) if chips % n == 0 and n * n <= chips)
     n_y = chips // n_x
-    cuts, n_w = pieces_uneven(tokens, (2, 4, 1, 1), 16), pieces_of(depth, 2, 16)
+    cuts, n_w = pieces_uneven(tokens, (6, 12, 2, 2, 2), 16), pieces_of(depth, 2, 16)
     n_a = len(cuts)
     held = pl.pallas_call(
         functools.partial(kernel, (n_y, n_x, n_col), (cuts, n_w)),

time: 29.8 us -> 29.6 us (level)
  no operation moved by 1% of the time
where the time goes in v3:
time: 29.6 us; the launch traced here: 29.4 us
  Pallas kernels  29.4 us (99%)
    pallas_call x1, Pallas kernels, body(): pl.pallas_call(functools.partial(kernel, (n_y, n_x, n_col), (cuts, n_w)),...  28.5 us
    pallas_call x1, Pallas kernels, body(): pl.pallas_call(functools.partial(finish, n_col, tokens - cuts[-1]), out_s...  0.95 us

profile of v3, /device:TPU:0, one launch (start us, length us, event | category | flops | bytes accessed | tf_op | source)
XLA Modules:
  0.0 29.4 jit_solution(12231863445128178222)
XLA Ops:
  0.0 28.5 %gather_up_silu.1 = (bf16[384,896]{1,0:T(8,128)(2,1)S(1)}, bf16[4,384,512]{2,1,0:T(8,128)(2,1)S(1)}, bf16[8,256,896]{2,1,0:T(8,128)(2,1)S(1)}, f32[384,896]{1,0:T(8,128)S(1)}) custom-call(bf16[384,512]{1,0:T(8,128)(2,1)} %a_hbm.1, bf16[256,896]{1,0:T(8,128)(2,1)} %w_hbm.1), custom_call_target="tpu_custom_call" | custom-call | flops 1409286144 | bytes 1540096 | tf_op jit(solution)/shard_map/gather_up_silu/pallas_call | solution.py:340
  28.5 1.0 %last_rows.1 = bf16[384,896]{1,0:T(8,128)(2,1)} custom-call(bf16[384,896]{1,0:T(8,128)(2,1)S(1)} %get-tuple-element.9.ready, bf16[4,384,512]{2,1,0:T(8,128)(2,1)S(1)} %get-tuple-element.10.acts, bf16[8,256,896]{2,1,0:T(8,128)(2,1)S(1)} %get-tuple-element.11.weights, f32[384,896]{1,0:T(8,128)S(1)} %get-tuple-element.12.total), custom_call_target="tpu_custom_call" | custom-call | tf_op jit(solution)/shard_map/last_rows/pallas_call | solution.py:370

commit v4 on v3

--- a/solution.py
+++ b/solution.py
@@ -164,8 +164,8 @@
     helped = jnp.where(r == 0, len(helpers), sum((jnp.where(r == helper, 1, 0) for helper, _ in helpers), 0))
     helped = jnp.where(c == 0, helped, 0)
 
-    own_a = pltpu.make_async_copy(a_hbm, acts.at[c], local_sem.at[0])
-    own_w = pltpu.make_async_copy(w_hbm, weights.at[0], local_sem.at[1])
+    own_a = pltpu.make_async_copy(a_hbm, acts.at[c], local_sem)
+    own_w = pltpu.make_async_copy(w_hbm, weights.at[0], share_w)
     own_a.start()
     own_w.start()
 
@@ -271,7 +271,7 @@
                 held_copy(held, there, (0, 0), send_h, recv_a.at[0, k]).start()
 
     events = [(0.4 * tokens * width, "out", 0, 0), (1.1 * tokens * width, "in", 0, 0)]
-    w_time, w_lag = row_w * hidden, tokens * width / 10
+    w_time, w_lag = row_w * hidden, tokens * width / 5
     for t in range(last):
         for k in range(n_a):
             events.append(((t // 2 * tokens + starts_a[k] + sizes_a[k]) * width, "a", t, k))
@@ -289,8 +289,7 @@
             first_weights(k)
         elif diagonal:
             far_weights(k)
-    filled(weights.at[pl.ds(0, n_row // 2)], share_w)
-    own_w.wait()
+    filled(weights.at[pl.ds(0, n_row // 2 + 1)], share_w)
     own_a.wait()
 
     product = functools.partial(product_of, n_col, c, acts, weights)
@@ -353,7 +352,7 @@
             pltpu.SemaphoreType.DMA,
             pltpu.SemaphoreType.DMA((2, n_w)),
             pltpu.SemaphoreType.DMA,
-            pltpu.SemaphoreType.DMA((2,)),
+            pltpu.SemaphoreType.DMA,
             pltpu.SemaphoreType.REGULAR,
             pltpu.VMEM((cuts[-1], width), jnp.bfloat16),
             pltpu.SemaphoreType.DMA,

time: 29.6 us -> 29.6 us (level)
  no operation moved by 1% of the time
where the time goes in v4:
time: 29.6 us; the launch traced here: 29.4 us
  Pallas kernels  29.4 us (99%)
    pallas_call x1, Pallas kernels, body(): pl.pallas_call(functools.partial(kernel, (n_y, n_x, n_col), (cuts, n_w)),...  28.5 us
    pallas_call x1, Pallas kernels, body(): pl.pallas_call(functools.partial(finish, n_col, tokens - cuts[-1]), out_s...  0.95 us

profile of v4, /device:TPU:0, one launch (start us, length us, event | category | flops | bytes accessed | tf_op | source)
XLA Modules:
  0.0 29.4 jit_solution(12942212397466570784)
XLA Ops:
  0.0 28.5 %gather_up_silu.1 = (bf16[384,896]{1,0:T(8,128)(2,1)S(1)}, bf16[4,384,512]{2,1,0:T(8,128)(2,1)S(1)}, bf16[8,256,896]{2,1,0:T(8,128)(2,1)S(1)}, f32[384,896]{1,0:T(8,128)S(1)}) custom-call(bf16[384,512]{1,0:T(8,128)(2,1)} %a_hbm.1, bf16[256,896]{1,0:T(8,128)(2,1)} %w_hbm.1), custom_call_target="tpu_custom_call" | custom-call | flops 1409286144 | bytes 1540096 | tf_op jit(solution)/shard_map/gather_up_silu/pallas_call | solution.py:339
  28.5 1.0 %last_rows.1 = bf16[384,896]{1,0:T(8,128)(2,1)} custom-call(bf16[384,896]{1,0:T(8,128)(2,1)S(1)} %get-tuple-element.9.ready, bf16[4,384,512]{2,1,0:T(8,128)(2,1)S(1)} %get-tuple-element.10.acts, bf16[8,256,896]{2,1,0:T(8,128)(2,1)S(1)} %get-tuple-element.11.weights, f32[384,896]{1,0:T(8,128)S(1)} %get-tuple-element.12.total), custom_call_target="tpu_custom_call" | custom-call | tf_op jit(solution)/shard_map/last_rows/pallas_call | solution.py:369
